TPU v7x, 32 devices: a whole 2x2x4 slice. The times are simulated.
32 devices in a mesh: shot: 8 (over z, y), off: 4 (over x, core).
Axes of the slice: x: 2, y: 2, z: 4, core: 2. Of those that a mesh axis runs over, the one named last changes fastest.
Arguments:
- traces: bfloat16 [32, 768, 2048], P('shot', 'off'), may hold values from -60 to 60
- offset_bin: int32 [32, 768], P('shot', 'off'), may hold values from 0 to 31, as said below
- rec_id: int32 [32, 768], P('shot', 'off'), may hold values from 0 to 2047, as said below
- cmp_id: int32 [32, 768], P('shot', 'off'), may hold values from 0 to 4095, as said below
- rec_owner: int32 [2048], replicated, may hold values from 0 to 7, as said below
- rec_slot: int32 [2048], replicated, may hold values from 0 to 255
- cmp_owner: int32 [4096], replicated, may hold values from 0 to 7, as said below
- cmp_slot: int32 [4096], replicated, may hold values from 0 to 511
Outputs:
- source_term: float32 [32, 640], P('shot')
- offset_term: float32 [32, 640], P('off')
- receiver_term: float32 [2048, 640], P(('shot', 'off'))
- midpoint_term: float32 [4096, 640], P(('shot', 'off'))
Inputs may be any that keep to these rules, and one draw needn't show every extreme that they name: `offset_bin`: a trace at position j of its shot has a bin of (j // 192) * 8 to (j // 192 + 1) * 8 - 1. rec_owner[r] * 256 + rec_slot[r] takes every value below 2048 exactly once. cmp_owner[c] * 512 + cmp_slot[c] takes every value below 4096 exactly once. `rec_id`: of the traces of one device's block (4 shots by 192 traces) at most 192 have receivers of any one owner; for every offset group some owner gets exactly 192 from every block of that group. `cmp_id`: of the traces of one device's block at most 192 have midpoints of any one owner; for every offset group some owner gets exactly 192 from every block of that group.
All inputs are finite; a program needn't handle non-finite values.
Results may differ from a plain program's by a relative error of at most 0.0035.
Values may be sent and summed in bfloat16 or wider, within the bound.
A program may use at most 64 MiB of HBM per device.

v0:
```python
import math

import jax
import jax.numpy as jnp
import numpy as np
from jax import lax
from jax.experimental import pallas as pl
from jax.experimental.pallas import tpu as pltpu
from jax.sharding import PartitionSpec as P

NF = 640
OFFB_DEV = 8
SWEEPS = 2
LANES = 128
WIDE = 256

OMEGA = 0.35
FLOOR = 0.05
VMEM_BYTES = 60 * 1024 * 1024


def up(value, unit):
    return -(-value // unit) * unit


def dot_nt(a, b):
    return lax.dot_general(a, b, (((1,), (1,)), ((), ())), preferred_element_type=jnp.float32)


def dot_nn(a, b):
    return lax.dot_general(a, b, (((1,), (0,)), ((), ())), preferred_element_type=jnp.float32)


def base_angles(samples, n_dev, held, padded):
    row = np.arange(n_dev * padded)
    freq = ((row // padded) * held + row % padded)[:, None]
    step = 2.0 * math.pi / samples
    coarse = freq * (np.arange(samples // LANES)[None, :] * LANES) % samples * step
    fine = freq * np.arange(LANES)[None, :] % samples * step
    tapers = 0.5 - 0.5 * np.cos((np.arange(samples)[None, :] + 0.5) * step)
    weights = tapers * math.sqrt(8.0 / (3.0 * samples))
    tables = (np.cos(coarse), np.sin(coarse), np.cos(fine), np.sin(fine), weights)
    return tuple(table.astype(np.float32) for table in tables)


def my_position(n_off):
    return lax.axis_index("shot") * n_off + lax.axis_index("off")


def remote(src, dst, send_sem, recv_sem, dest, n_off):
    return pltpu.make_async_remote_copy(
        src_ref=src,
        dst_ref=dst,
        send_sem=send_sem,
        recv_sem=recv_sem,
        device_id=(dest // n_off, dest % n_off),
        device_id_type=pl.DeviceIdType.MESH,
    )


def greet_all(me, n_dev, n_off):
    barrier = pltpu.get_barrier_semaphore()

    @pl.loop(1, n_dev)
    def _(step):
        dest = (me + step) % n_dev
        pl.semaphore_signal(
            barrier,
            inc=1,
            device_id=(dest // n_off, dest % n_off),
            device_id_type=pl.DeviceIdType.MESH,
        )

    return barrier


def send_logs(n_off, groups, held, traces_ref, id_refs, table_refs, landed, bins, scratch):
    ca_ref, sa_ref, cb_ref, sb_ref, w_ref = table_refs
    stage, own_bins, id_rows, table, send_sems, recv_sems, bin_send_sems, bin_recv_sems, own_sems = (
        scratch
    )
    n_dev, padded, tr_dev = landed.shape
    dests = n_dev // groups
    rows = dests * padded
    me = my_position(n_off)
    barrier = greet_all(me, n_dev, n_off)
    bin_ref, rec_ref, cmp_ref = id_refs
    shot_dev, tr_off = bin_ref.shape
    id_rows[...] = jnp.zeros_like(id_rows)
    for shot in range(shot_dev):
        cols = slice(shot * tr_off, (shot + 1) * tr_off)
        own_bins[:, cols] = bin_ref[shot : shot + 1, :]
        rec = rec_ref[shot : shot + 1, :]
        cmp = cmp_ref[shot : shot + 1, :]
        parts = (rec % WIDE, rec // WIDE, cmp % WIDE, cmp // WIDE)
        for k, part in enumerate(parts):
            id_rows[held + k : held + k + 1, cols] = part.astype(jnp.float32)

    def block_copy(dest, slot):
        return remote(
            stage.at[dest], landed.at[slot], send_sems.at[dest], recv_sems.at[slot], dest, n_off
        )

    def bin_copy(dest, slot):
        return remote(
            own_bins, bins.at[slot], bin_send_sems.at[dest], bin_recv_sems.at[slot], dest, n_off
        )

    def turn_group(turn):
        if groups & (groups - 1) == 0:
            return (me // dests) ^ (groups - 1 - turn)
        return ((me // dests) + groups - 1 - turn) % groups

    own_copy = pltpu.make_async_copy(own_bins, bins.at[me], own_sems.at[0])
    own_copy.start()
    freq_row = lax.broadcasted_iota(jnp.int32, (dests, padded, tr_dev), 1)
    for turn in range(groups):
        group = turn_group(turn)
        base = pl.multiple_of(group * rows, 8)
        cb = cb_ref[pl.ds(base, rows), :]
        sb = sb_ref[pl.ds(base, rows), :]
        ca_all = ca_ref[pl.ds(base, rows), :]
        sa_all = sa_ref[pl.ds(base, rows), :]
        for a in range(traces_ref.shape[1] // LANES):
            cols = slice(a * LANES, (a + 1) * LANES)
            w = w_ref[:, cols]
            ca = ca_all[:, a : a + 1]
            sa = sa_all[:, a : a + 1]
            table[:rows, cols] = (w * (ca * cb - sa * sb)).astype(jnp.bfloat16)
            table[rows:, cols] = (-w * (sa * cb + ca * sb)).astype(jnp.bfloat16)
        products = dot_nt(table[...], traces_ref[...])
        real_part = products[:rows]
        imag_part = products[rows:]
        logs = jnp.log(real_part * real_part + imag_part * imag_part + FLOOR)
        logs = logs.reshape(dests, padded, tr_dev)
        logs = jnp.where(freq_row < held, logs, id_rows[...][None])
        stage[pl.ds(group * dests, dests)] = logs.astype(jnp.bfloat16)
        if turn == 0:
            pl.semaphore_wait(barrier, n_dev - 1)

        @pl.loop(0, dests)
        def _(step):
            dest = group * dests + (step + me) % dests

            @pl.when(dest != me)
            def _():
                block_copy(dest, me).start()
                bin_copy(dest, me).start()

    own = pltpu.make_async_copy(stage.at[me], landed.at[me], own_sems.at[1])
    own.start()
    own_copy.wait()
    own.wait()

    def arrival(turn, step):
        src = turn_group(turn) * dests + (me + dests - step) % dests

        @pl.when(src != me)
        def _():
            block_copy(src, src).wait_recv()
            bin_copy(src, src).wait_recv()

        return src

    def finish():
        @pl.loop(1, n_dev)
        def _(step):
            dest = (me + step) % n_dev
            block_copy(dest, me).wait_send()
            bin_copy(dest, me).wait_send()

    return arrival, finish


def return_kernel(
    n_off,
    splits,
    terms_ref,
    source_ref,
    offset_ref,
    rec_ref,
    cmp_ref,
    landed,
    joined,
    send_sems,
    recv_sems,
    own_sem,
):
    n_dev = terms_ref.shape[0]
    held = -(-source_ref.shape[1] // n_dev)
    me = my_position(n_off)
    barrier = greet_all(me, n_dev, n_off)

    def block_copy(dest, slot):
        return remote(
            terms_ref.at[dest], landed.at[slot], send_sems.at[dest], recv_sems.at[slot], dest, n_off
        )

    own = pltpu.make_async_copy(terms_ref.at[me], landed.at[me], own_sem)
    own.start()
    pl.semaphore_wait(barrier, n_dev - 1)

    @pl.loop(1, n_dev)
    def _(step):
        block_copy((me + step) % n_dev, me).start()

    @pl.loop(1, n_dev)
    def _(step):
        dest = (me + step) % n_dev
        block_copy(dest, me).wait_send()
        block_copy(dest, dest).wait_recv()

    own.wait()
    for src in range(n_dev):
        rows = min(held, joined.shape[0] - src * held)
        if rows > 0:
            joined[src * held : src * held + rows, :] = landed[src].astype(jnp.float32)[:rows]
    turned = joined[...].T
    a, b, c, d = splits
    rec_ref[...] = turned[:a]
    cmp_ref[...] = turned[a:b]
    offset_ref[...] = turned[b:c]
    source_ref[...] = turned[c:d]


def return_terms(terms, n_off, splits):
    n_dev, padded, columns = terms.shape
    a, b, c, d = splits
    vmem = pl.BlockSpec(memory_space=pltpu.VMEM)
    shape = lambda rows: jax.ShapeDtypeStruct((rows, NF), jnp.float32)
    return pl.pallas_call(
        lambda *refs: return_kernel(n_off, splits, *refs),
        out_shape=(shape(d - c), shape(c - b), shape(a), shape(b - a)),
        in_specs=[vmem],
        out_specs=(vmem,) * 4,
        scratch_shapes=[
            pltpu.VMEM((n_dev, padded, columns), jnp.bfloat16),
            pltpu.VMEM((NF, columns), jnp.float32),
            pltpu.SemaphoreType.DMA((n_dev,)),
            pltpu.SemaphoreType.DMA((n_dev,)),
            pltpu.SemaphoreType.DMA,
        ],
        compiler_params=pltpu.CompilerParams(
            vmem_limit_bytes=VMEM_BYTES, collective_id=1, has_side_effects=True
        ),
        name="returns",
    )(terms)


def one_hot(index, count):
    rows = lax.broadcasted_iota(jnp.int32, (count, index.shape[1]), 0)
    return jnp.where(rows.astype(index.dtype) == index, 1.0, 0.0).astype(jnp.bfloat16)


def level_mask(index, levels, rows):
    level = lax.broadcasted_iota(jnp.int32, (levels, rows, index.shape[1]), 0)
    return level.astype(index.dtype) == index[None]


def spread(values, mask):
    levels, rows, width = mask.shape
    return jnp.where(mask, values[None], 0.0).astype(jnp.bfloat16).reshape(levels * rows, width)


def split_float(values):
    high = values.astype(jnp.bfloat16)
    low = (values - high.astype(jnp.float32)).astype(jnp.bfloat16)
    return jnp.concatenate([high, low], axis=0)


def sweeps_kernel(
    sizes,
    traces_ref,
    bin_ref,
    rec_ref,
    cmp_ref,
    ca_ref,
    sa_ref,
    cb_ref,
    sb_ref,
    w_ref,
    rec_owner_ref,
    rec_slot_ref,
    cmp_owner_ref,
    cmp_slot_ref,
    out_ref,
    landed,
    bins,
    rec_acc,
    cmp_acc,
    so_acc,
    rec_x,
    cmp_x,
    so_x,
    rec_b,
    cmp_b,
    placed,
    *send_scratch,
):
    n_shot, n_off, shot_dev, held, rec_dev, cmp_dev = sizes
    n_dev, padded, tr_dev = landed.shape
    groups = 4 if n_dev % 4 == 0 else 1
    dests = n_dev // groups
    tr_off = tr_dev // shot_dev
    n_bins = n_off * OFFB_DEV
    rec_l = rec_acc.shape[0] // padded
    cmp_l = cmp_acc.shape[0] // padded
    so_width = so_acc.shape[1]
    freq_row = lax.broadcasted_iota(jnp.int32, (padded, tr_dev), 0)
    local_shot = lax.broadcasted_iota(jnp.int32, (1, tr_dev), 1) // tr_off
    arrival, finish = send_logs(
        n_off,
        groups,
        held,
        traces_ref,
        (bin_ref, rec_ref, cmp_ref),
        (ca_ref, sa_ref, cb_ref, sb_ref, w_ref),
        landed,
        bins,
        send_scratch,
    )

    def add_source(src, first):
        values = landed[src].astype(jnp.float32)
        rec_h, rec_level, cmp_h, cmp_level = (
            values[held + k : held + k + 1] for k in range(4)
        )
        shot = (src // n_off) * shot_dev + local_shot + n_bins
        so_row = lax.broadcasted_iota(jnp.int32, (so_width, tr_dev), 0)
        so_hot = jnp.where((so_row == bins[src]) | (so_row == shot), 1.0, 0.0).astype(jnp.bfloat16)
        rec_hot = one_hot(rec_h, WIDE)
        cmp_hot = one_hot(cmp_h, WIDE)
        rec_mask = level_mask(rec_level, rec_l, padded)
        cmp_mask = level_mask(cmp_level, cmp_l, padded)
        if first:
            values = jnp.where(freq_row == held, 1.0, values)
        else:
            so_part = dot_nn(so_x[...], so_hot)
            rec_part = dot_nn(rec_x[...], rec_hot).reshape(rec_mask.shape)
            cmp_part = dot_nn(cmp_x[...], cmp_hot).reshape(cmp_mask.shape)
            values = values - (so_part[:padded] + so_part[padded:])
            values = values - jnp.sum(jnp.where(rec_mask, rec_part, 0.0), axis=0)
            values = values - jnp.sum(jnp.where(cmp_mask, cmp_part, 0.0), axis=0)
        rec_acc[...] += dot_nt(spread(values, rec_mask), rec_hot)
        cmp_acc[...] += dot_nt(spread(values, cmp_mask), cmp_hot)
        so_acc[...] += dot_nt(values.astype(jnp.bfloat16), so_hot)

    def sums_over_traces(first):
        rec_acc[...] = jnp.zeros_like(rec_acc)
        cmp_acc[...] = jnp.zeros_like(cmp_acc)
        so_acc[...] = jnp.zeros_like(so_acc)
        if not first:

            @pl.loop(0, n_dev)
            def _(src):
                add_source(src, False)

            return
        @pl.loop(0, n_dev)
        def _(step):
            add_source(arrival(step // dests, step % dests), True)

        finish()

    def update(sums, counts, levels):
        shaped = sums.reshape(levels, padded, sums.shape[1])
        number = counts.reshape(shaped.shape)[:, held : held + 1, :]
        return OMEGA * shaped / (number + 1.0)

    sums_over_traces(True)
    rec_counts, cmp_counts, so_counts = rec_b, cmp_b, placed
    rec_counts[...] = rec_acc[...]
    cmp_counts[...] = cmp_acc[...]
    so_first = update(so_acc[...], so_acc[...], 1).reshape(padded, so_width)
    so_number = so_acc[held : held + 1, :]
    rec_x[...] = update(rec_acc[...], rec_acc[...], rec_l).reshape(rec_x.shape).astype(jnp.bfloat16)
    cmp_x[...] = update(cmp_acc[...], cmp_acc[...], cmp_l).reshape(cmp_x.shape).astype(jnp.bfloat16)
    so_x[...] = split_float(so_first)
    for _ in range(SWEEPS - 1):
        sums_over_traces(False)
    rec_acc[...] = update(rec_acc[...] + rec_counts[...], rec_counts[...], rec_l).reshape(
        rec_acc.shape
    )
    cmp_acc[...] = update(cmp_acc[...] + cmp_counts[...], cmp_counts[...], cmp_l).reshape(
        cmp_acc.shape
    )
    so_final = so_first + OMEGA * so_acc[...] / (so_number + 1.0)

    rec_rows = rec_dev // n_off
    cmp_rows = cmp_dev // n_off
    columns = out_ref.shape[2]
    placed[...] = jnp.zeros_like(placed)

    def place(values, dest, column):
        mask = level_mask(dest, n_dev, padded)
        placed[...] += dot_nt(spread(values, mask), one_hot(column, columns))

    @pl.loop(0, rec_l)
    def _(level):
        span = pl.ds(pl.multiple_of(level * WIDE, WIDE), WIDE)
        position = (rec_owner_ref[span] * rec_dev + rec_slot_ref[span]).reshape(1, WIDE)
        values = rec_acc[pl.ds(pl.multiple_of(level * padded, 8), padded), :]
        place(values, position // rec_rows, position % rec_rows)

    @pl.loop(0, cmp_l)
    def _(level):
        span = pl.ds(pl.multiple_of(level * WIDE, WIDE), WIDE)
        position = (cmp_owner_ref[span] * cmp_dev + cmp_slot_ref[span]).reshape(1, WIDE)
        values = cmp_acc[pl.ds(pl.multiple_of(level * padded, 8), padded), :]
        place(values, position // cmp_rows, position % cmp_rows + rec_rows)

    item = lax.broadcasted_iota(jnp.int32, (1, so_width), 1)
    shot = item - n_bins
    is_bin = item < n_bins
    base = rec_rows + cmp_rows
    column = jnp.where(is_bin, base + item % OFFB_DEV, base + OFFB_DEV + shot % shot_dev)
    dest = lax.broadcasted_iota(jnp.int32, (n_dev, padded, so_width), 0)
    items = lax.broadcasted_iota(jnp.int32, (n_dev, padded, so_width), 2)
    mask = jnp.where(items < n_bins, dest % n_off, dest // n_off) == jnp.where(
        items < n_bins, items // OFFB_DEV, (items - n_bins) // shot_dev
    )
    placed[...] += dot_nt(spread(so_final, mask), one_hot(column, columns))
    out_ref[...] = placed[...].astype(jnp.bfloat16).reshape(out_ref.shape)


def run_sweeps(traces, ids, owners, sizes, padded, columns):
    n_shot, n_off, shot_dev, held, _, _ = sizes
    n_dev = n_shot * n_off
    tr_dev, samples = traces.shape
    groups = 4 if n_dev % 4 == 0 else 1
    rows = n_dev // groups * padded
    rec_l = owners[0].shape[0] // WIDE
    cmp_l = owners[2].shape[0] // WIDE
    so_width = up(n_shot * shot_dev + n_off * OFFB_DEV, LANES)
    tables = base_angles(samples, n_dev, held, padded)
    vmem = pl.BlockSpec(memory_space=pltpu.VMEM)
    return pl.pallas_call(
        lambda *refs: sweeps_kernel(sizes, *refs),
        out_shape=jax.ShapeDtypeStruct((n_dev, padded, columns), jnp.bfloat16),
        in_specs=[vmem] * 13,
        out_specs=vmem,
        scratch_shapes=[
            pltpu.VMEM((n_dev, padded, tr_dev), jnp.bfloat16),
            pltpu.VMEM((n_dev, 1, tr_dev), jnp.int32),
            pltpu.VMEM((rec_l * padded, WIDE), jnp.float32),
            pltpu.VMEM((cmp_l * padded, WIDE), jnp.float32),
            pltpu.VMEM((padded, so_width), jnp.float32),
            pltpu.VMEM((rec_l * padded, WIDE), jnp.bfloat16),
            pltpu.VMEM((cmp_l * padded, WIDE), jnp.bfloat16),
            pltpu.VMEM((2 * padded, so_width), jnp.bfloat16),
            pltpu.VMEM((rec_l * padded, WIDE), jnp.float32),
            pltpu.VMEM((cmp_l * padded, WIDE), jnp.float32),
            pltpu.VMEM((n_dev * padded, columns), jnp.float32),
            pltpu.VMEM((n_dev, padded, tr_dev), jnp.bfloat16),
            pltpu.VMEM((1, tr_dev), jnp.int32),
            pltpu.VMEM((padded, tr_dev), jnp.float32),
            pltpu.VMEM((2 * rows, samples), jnp.bfloat16),
            pltpu.SemaphoreType.DMA((n_dev,)),
            pltpu.SemaphoreType.DMA((n_dev,)),
            pltpu.SemaphoreType.DMA((n_dev,)),
            pltpu.SemaphoreType.DMA((n_dev,)),
            pltpu.SemaphoreType.DMA((2,)),
        ],
        compiler_params=pltpu.CompilerParams(
            vmem_limit_bytes=VMEM_BYTES, collective_id=0, has_side_effects=True
        ),
        name="sweeps",
    )(traces, *ids, *tables, *owners)


def shards(traces, offset_bin, rec_id, cmp_id, rec_owner, rec_slot, cmp_owner, cmp_slot):
    shot_dev, tr_off, samples = traces.shape
    n_shot = lax.axis_size("shot")
    n_off = lax.axis_size("off")
    n_dev = n_shot * n_off
    tr_dev = shot_dev * tr_off
    rec_dev = rec_owner.shape[0] // n_shot
    cmp_dev = cmp_owner.shape[0] // n_shot
    rec_rows = rec_dev // n_off
    cmp_rows = cmp_dev // n_off
    held = up(NF, n_dev) // n_dev
    padded = up(held + 4, 8)
    columns = up(rec_rows + cmp_rows + shot_dev + OFFB_DEV, LANES)
    terms = run_sweeps(
        traces.reshape(tr_dev, samples),
        (offset_bin, rec_id, cmp_id),
        (rec_owner, rec_slot, cmp_owner, cmp_slot),
        (n_shot, n_off, shot_dev, held, rec_dev, cmp_dev),
        padded,
        columns,
    )
    base = rec_rows + cmp_rows
    splits = (rec_rows, base, base + OFFB_DEV, base + OFFB_DEV + shot_dev)
    return return_terms(terms, n_off, splits)


def solution(mesh):
    return jax.shard_map(
        shards,
        mesh=mesh,
        in_specs=(
            P("shot", "off", None),
            P("shot", "off"),
            P("shot", "off"),
            P("shot", "off"),
            P(),
            P(),
            P(),
            P(),
        ),
        out_specs=(
            P("shot", None),
            P("off", None),
            P(("shot", "off"), None),
            P(("shot", "off"), None),
        ),
        check_vma=False,
    )
```

profile of v0, /device:TPU:0, one launch (start us, length us, event | category | flops | bytes accessed | tf_op | source)
XLA Modules:
  0.0 107.8 jit_solution(7108909261788641729)
XLA Ops:
  0.6 88.0 %sweeps.1.refs_0_ = bf16[32,24,256]{2,1,0:T(8,128)(2,1)} custom-call(bf16[768,2048]{1,0:T(8,128)(2,1)} %bitcast.1, s32[4,192]{1,0:T(4,128)} %refs_1_.1, s32[4,192]{1,0:T(4,128)} %refs_2_.1, s32[4,192]{1,0:T(4,128)} %refs_3_.1, f32[768,16]{1,0:T(8,128)} %constant.10.clone.refs_4_, f32[768,16]{1,0:T(8,128)} %constant.11.clone.refs_5_, ...), custom_call_target="tpu_custom_call" | custom-call | tf_op jit(solution)/shard_map/sweeps/pallas_call | solution.py:437
  88.7 13.1 %returns.1 = (f32[4,640]{1,0:T(4,128)}, f32[8,640]{1,0:T(8,128)}, f32[64,640]{1,0:T(8,128)}, f32[128,640]{1,0:T(8,128)}) custom-call(bf16[32,24,256]{2,1,0:T(8,128)(2,1)} %sweeps.1.refs_0_), custom_call_target="tpu_custom_call" | custom-call | tf_op jit(solution)/shard_map/returns/pallas_call | solution.py:231
  101.8 1.3 %copy.21 = f32[4,640]{1,0:T(4,128)} copy(f32[4,640]{1,0:T(4,128)} %get-tuple-element.8) | data formatting | bytes 20480
  103.1 1.3 %copy.22 = f32[8,640]{1,0:T(8,128)} copy(f32[8,640]{1,0:T(8,128)} %get-tuple-element.9) | data formatting | bytes 40960
  104.4 1.6 %copy.23 = f32[64,640]{1,0:T(8,128)} copy(f32[64,640]{1,0:T(8,128)} %get-tuple-element.10) | data formatting | bytes 327680
  106.0 1.7 %copy.24 = f32[128,640]{1,0:T(8,128)} copy(f32[128,640]{1,0:T(8,128)} %get-tuple-element.11) | data formatting | bytes 655360
where the time goes:
time: 109 us; the launch traced here: 108 us
  Pallas kernels  101 us (93%)
  local copies, waits for them, and re-layouts  5.95 us (5%)
    pallas_call x1, Pallas kernels, run_sweeps(): pl.pallas_call(lambda *refs: sweeps_kernel(sizes, *refs), out_shape=jax.S...  88 us
    pallas_call x1, Pallas kernels, return_terms(): pl.pallas_call(lambda *refs: return_kernel(n_off, splits, *refs), out_sha...  13.1 us
    unnamed x4, local copies, waits for them, and re-layouts  5.95 us

commit v1 on v0

v1 whole, which is shorter than its diff:
```python
import math

import jax
import jax.numpy as jnp
import numpy as np
from jax import lax
from jax.experimental import pallas as pl
from jax.experimental.pallas import tpu as pltpu
from jax.sharding import PartitionSpec as P

NF = 640
OFFB_DEV = 8
SWEEPS = 2
LANES = 128
WIDE = 256
REM = 4
ITEMS = 16
ID_ROWS = 8

OMEGA = 0.35
FLOOR = 0.05
VMEM_BYTES = 60 * 1024 * 1024
HOT_BYTES = 40 * 1024 * 1024


def up(value, unit):
    return -(-value // unit) * unit


def dot_nt(a, b):
    return lax.dot_general(a, b, (((1,), (1,)), ((), ())), preferred_element_type=jnp.float32)


def dot_nn(a, b):
    return lax.dot_general(a, b, (((1,), (0,)), ((), ())), preferred_element_type=jnp.float32)


def group_count(n_dev):
    return 4 if n_dev % 4 == 0 else 1


def base_angles(samples, n_dev, held, main):
    groups = group_count(n_dev)
    dests = n_dev // groups
    rows = dests * (main + REM)
    row = np.arange(groups * rows)
    group, inside = row // rows, row % rows
    in_main = inside < dests * main
    rest = inside - dests * main
    dest = np.where(in_main, inside // max(main, 1), rest // REM)
    place = np.where(in_main, inside % max(main, 1), main + rest % REM)
    freq = ((group * dests + dest) * held + place)[:, None]
    step = 2.0 * math.pi / samples
    coarse = freq * (np.arange(samples // LANES)[None, :] * LANES) % samples * step
    fine = freq * np.arange(LANES)[None, :] % samples * step
    tapers = 0.5 - 0.5 * np.cos((np.arange(samples)[None, :] + 0.5) * step)
    weights = tapers * math.sqrt(8.0 / (3.0 * samples))
    tables = (np.cos(coarse), np.sin(coarse), np.cos(fine), np.sin(fine), weights)
    return tuple(table.astype(np.float32) for table in tables)


def remote(src, dst, send_sem, recv_sem, dest, n_off):
    return pltpu.make_async_remote_copy(
        src_ref=src,
        dst_ref=dst,
        send_sem=send_sem,
        recv_sem=recv_sem,
        device_id=(dest // n_off, dest % n_off),
        device_id_type=pl.DeviceIdType.MESH,
    )


def greet_all(me, n_dev, n_off):
    barrier = pltpu.get_barrier_semaphore()

    @pl.loop(1, n_dev)
    def _(step):
        dest = (me + step) % n_dev
        pl.semaphore_signal(
            barrier,
            inc=1,
            device_id=(dest // n_off, dest % n_off),
            device_id_type=pl.DeviceIdType.MESH,
        )

    return barrier


def lower_half(shape):
    return lax.broadcasted_iota(jnp.int32, shape, 0) >= REM


def fold(values):
    return values + pltpu.roll(values, REM, 0)


def terms_kernel(
    sizes,
    traces_ref,
    bin_ref,
    rec_ref,
    cmp_ref,
    ca_ref,
    sa_ref,
    cb_ref,
    sb_ref,
    w_ref,
    rec_owner_ref,
    rec_slot_ref,
    cmp_owner_ref,
    cmp_slot_ref,
    out_ref,
    stage,
    landed,
    table,
    raw,
    id_rows,
    ids,
    rec_tab,
    cmp_tab,
    iota_ref,
    hots,
    rec_acc,
    cmp_acc,
    rec_cnt,
    cmp_cnt,
    so_acc,
    rec_x,
    cmp_x,
    so_x,
    ret_stage,
    ret_landed,
    send_sems,
    recv_sems,
    line_send_sems,
    line_recv_sems,
    layer_send_sems,
    layer_recv_sems,
    ret_send_sems,
    ret_recv_sems,
    own_sems,
):
    n_shot, n_off, shot_dev, tr_off, rec_dev, cmp_dev, main = sizes
    n_dev = n_shot * n_off
    groups = group_count(n_dev)
    dests = n_dev // groups
    rows = dests * (main + REM)
    tr_dev, samples = traces_ref.shape
    half = tr_dev // 2
    rec_l = rec_cnt.shape[0]
    cmp_l = cmp_cnt.shape[0]
    rec_rows = rec_dev // n_off
    cmp_rows = cmp_dev // n_off
    keep_hots = hots.shape[0] == n_dev
    me = lax.axis_index("shot") * n_off + lax.axis_index("off")
    my_group = me // dests
    my_place = me % dests
    barrier = greet_all(me, n_dev, n_off)

    def block_copy(dest, slot):
        return remote(
            stage.at[dest], landed.at[slot], send_sems.at[dest], recv_sems.at[slot], dest, n_off
        )

    def line_copy(step, slot):
        block = ids.at[my_place, slot]
        dest = (my_group ^ step) * dests + my_place
        return remote(block, block, line_send_sems.at[step], line_recv_sems.at[step], dest, n_off)

    def layer_copy(place, slot):
        block = ids.at[slot]
        dest = my_group * dests + place
        return remote(block, block, layer_send_sems.at[place], layer_recv_sems.at[slot], dest, n_off)

    def return_copy(dest, slot):
        return remote(
            ret_stage.at[dest],
            ret_landed.at[slot],
            ret_send_sems.at[dest],
            ret_recv_sems.at[slot],
            dest,
            n_off,
        )

    def stage_logs(group):
        base = pl.multiple_of(group * rows, 8)
        cb = cb_ref[pl.ds(base, rows), :]
        sb = sb_ref[pl.ds(base, rows), :]
        ca_all = ca_ref[pl.ds(base, rows), :]
        sa_all = sa_ref[pl.ds(base, rows), :]
        for a in range(samples // LANES):
            cols = slice(a * LANES, (a + 1) * LANES)
            w = w_ref[:, cols]
            ca = ca_all[:, a : a + 1]
            sa = sa_all[:, a : a + 1]
            table[:rows, cols] = (w * (ca * cb - sa * sb)).astype(jnp.bfloat16)
            table[rows:, cols] = (-w * (sa * cb + ca * sb)).astype(jnp.bfloat16)
        products = dot_nt(table[...], traces_ref[...])
        real_part = products[:rows]
        imag_part = products[rows:]
        logs = jnp.log(real_part * real_part + imag_part * imag_part + FLOOR)
        first = group * dests
        if main:
            block = logs[: dests * main].reshape(dests, main, tr_dev).astype(jnp.bfloat16)
            stage[pl.ds(first, dests), :main, :] = block[:, :, :half]
            stage[pl.ds(first, dests), main : 2 * main, :] = block[:, :, half:]
        rest = logs[dests * main :]
        low = lower_half((2 * REM, half))
        for pair in range(dests // 2):
            both = rest[2 * REM * pair : 2 * REM * (pair + 1)]
            left, right = both[:, :half], both[:, half:]
            upper = jnp.where(low, pltpu.roll(right, REM, 0), left)
            lower = jnp.where(low, right, pltpu.roll(left, REM, 0))
            stage[first + 2 * pair, 2 * main :, :] = upper.astype(jnp.bfloat16)
            stage[first + 2 * pair + 1, 2 * main :, :] = lower.astype(jnp.bfloat16)

    def send_group(group, own):
        @pl.loop(1 if own else 0, dests)
        def _(step):
            block_copy(group * dests + (step + my_place) % dests, me).start()

    def one_hot_f32(index):
        row = lax.broadcasted_iota(jnp.int32, (WIDE, index.shape[1]), 0)
        return jnp.where(row == index, 1.0, 0.0).astype(jnp.bfloat16)

    def fill_table(tab, owner_ref, slot_ref, count_dev, levels):
        @pl.loop(0, levels)
        def _(level):
            span = pl.ds(pl.multiple_of(level * WIDE, WIDE), WIDE)
            position = (owner_ref[span] * count_dev + slot_ref[span]).reshape(1, WIDE)
            tab[pl.ds(level, 1), :] = (position // WIDE).astype(jnp.float32)
            tab[pl.ds(levels + level, 1), :] = (position % WIDE).astype(jnp.float32)

    def look_up(index, tab, levels):
        part = dot_nn(tab[...].astype(jnp.bfloat16), one_hot_f32(index % WIDE))
        level = lax.broadcasted_iota(jnp.int32, (levels, index.shape[1]), 0)
        mask = level == index // WIDE
        high = jnp.sum(jnp.where(mask, part[:levels], 0.0), axis=0, keepdims=True)
        low = jnp.sum(jnp.where(mask, part[levels:], 0.0), axis=0, keepdims=True)
        return low, high

    def own_ids():
        fill_table(rec_tab, rec_owner_ref, rec_slot_ref, rec_dev, rec_l)
        fill_table(cmp_tab, cmp_owner_ref, cmp_slot_ref, cmp_dev, cmp_l)
        for shot in range(shot_dev):
            cols = slice(shot * tr_off, (shot + 1) * tr_off)
            raw[0:1, cols] = rec_ref[shot : shot + 1, :]
            raw[1:2, cols] = cmp_ref[shot : shot + 1, :]
            raw[2:3, cols] = bin_ref[shot : shot + 1, :]
        id_rows[...] = jnp.zeros_like(id_rows)
        id_rows[0:1, :], id_rows[1:2, :] = look_up(raw[0:1, :], rec_tab, rec_l)
        id_rows[2:3, :], id_rows[3:4, :] = look_up(raw[1:2, :], cmp_tab, cmp_l)
        id_rows[4:5, :] = (raw[2:3, :] % OFFB_DEV).astype(jnp.float32)
        ids[my_place, my_group] = id_rows[...].astype(jnp.bfloat16)

    def send_line():
        for step in range(1, groups):
            line_copy(step, my_group).start()

    def send_layer():
        for step in range(1, groups):
            line_copy(step, my_group ^ step).wait_recv()

        @pl.loop(1, dests)
        def _(step):
            layer_copy((my_place + step) % dests, my_place).start()

    row_lane = lax.broadcasted_iota(jnp.int32, (WIDE, LANES), 0)
    iota_ref[...] = row_lane.astype(jnp.float32).astype(jnp.bfloat16)
    rec_acc[...] = jnp.zeros_like(rec_acc)
    cmp_acc[...] = jnp.zeros_like(cmp_acc)
    rec_cnt[...] = jnp.zeros_like(rec_cnt)
    cmp_cnt[...] = jnp.zeros_like(cmp_cnt)
    so_acc[...] = jnp.zeros_like(so_acc)

    turns = [3, 0, 2, 1] if groups == 4 else [0]
    for turn, mask in enumerate(turns):
        stage_logs(my_group ^ mask)
        if turn == 0:
            pl.semaphore_wait(barrier, n_dev - 1)
        send_group(my_group ^ mask, mask == 0)
        if turn == 0:
            own_ids()
            send_line()
        if turn == min(1, groups - 1):
            send_layer()
    own = pltpu.make_async_copy(stage.at[me], landed.at[me], own_sems.at[0])
    own.start()
    own.wait()

    @pl.loop(1, dests)
    def _(step):
        place = (my_place + dests - step) % dests
        layer_copy(place, place).wait_recv()

    chunks = main // 8
    low_full = lower_half((2 * REM, tr_dev))
    low_half = lower_half((2 * REM, half))
    local_shot = lax.broadcasted_iota(jnp.int32, (ITEMS, tr_dev), 1) // tr_off
    item_row = lax.broadcasted_iota(jnp.int32, (ITEMS, tr_dev), 0)
    shot_hot = item_row - OFFB_DEV == local_shot

    def make_hot(index):
        column = index.astype(jnp.bfloat16)
        one = jnp.ones((), jnp.bfloat16)
        zero = jnp.zeros((), jnp.bfloat16)
        parts = []
        for a in range(tr_dev // LANES):
            cols = slice(a * LANES, (a + 1) * LANES)
            parts.append(jnp.where(iota_ref[...] == column[:, cols], one, zero))
        return jnp.concatenate(parts, axis=1)

    def level_masks(index, levels):
        level = jnp.broadcast_to(index, (8, tr_dev))
        odd = jnp.where(low_full, level - 1.0, level)
        return (
            lambda l: level == float(l),
            lambda pair: odd == float(2 * pair),
        )

    def spread(mains, rest, index, levels):
        is_level, is_pair = level_masks(index, levels)
        parts = []
        if chunks:
            for l in range(levels):
                mask = is_level(l)
                parts += [jnp.where(mask, part, 0.0) for part in mains]
        for pair in range(levels // 2):
            parts.append(jnp.where(is_pair(pair), rest, 0.0))
        return parts

    def gather(part, index, levels):
        is_level, is_pair = level_masks(index, levels)
        mains = [0.0] * chunks
        if chunks:
            for l in range(levels):
                mask = is_level(l)
                for c in range(chunks):
                    start = l * main + 8 * c
                    mains[c] = mains[c] + jnp.where(mask, part[start : start + 8], 0.0)
        rest = 0.0
        for pair in range(levels // 2):
            start = levels * main + 8 * pair
            rest = rest + jnp.where(is_pair(pair), part[start : start + 8], 0.0)
        return mains, fold(rest)

    def add_source(src, first):
        block = landed[src].astype(jnp.float32)
        rest = block[2 * main :]
        turned = pltpu.roll(rest, REM, 0)
        rest = jnp.concatenate(
            [jnp.where(low_half, turned, rest), jnp.where(low_half, rest, turned)], axis=1
        )
        mains = [
            jnp.concatenate(
                [block[8 * c : 8 * c + 8], block[main + 8 * c : main + 8 * c + 8]], axis=1
            )
            for c in range(chunks)
        ]
        keys = ids[src % dests, src // dests].astype(jnp.float32)
        rec_low, rec_high, cmp_low, cmp_high, bins = (keys[k : k + 1] for k in range(5))
        so_hot = (item_row.astype(jnp.float32) == bins) | shot_hot
        so_hot = jnp.where(so_hot, 1.0, 0.0).astype(jnp.bfloat16)
        if first or not keep_hots:
            rec_hot = make_hot(rec_low)
            cmp_hot = make_hot(cmp_low)
            if keep_hots:
                hots[src, 0] = rec_hot
                hots[src, 1] = cmp_hot
        else:
            rec_hot = hots[src, 0]
            cmp_hot = hots[src, 1]
        if not first:
            so_part = dot_nn(so_x[src][:, :ITEMS], so_hot)
            held = main + 2 * REM
            so_part = so_part[:held] + so_part[held:]
            rec_mains, rec_rest = gather(dot_nn(rec_x[...], rec_hot), rec_high, rec_l)
            cmp_mains, cmp_rest = gather(dot_nn(cmp_x[...], cmp_hot), cmp_high, cmp_l)
            for c in range(chunks):
                mains[c] = mains[c] - so_part[8 * c : 8 * c + 8] - rec_mains[c] - cmp_mains[c]
            rest = rest - so_part[main:] - rec_rest - cmp_rest
        rec_parts = spread(mains, rest, rec_high, rec_l)
        cmp_parts = spread(mains, rest, cmp_high, cmp_l)
        so_parts = mains + [rest]
        if first:
            for parts, index, levels in ((rec_parts, rec_high, rec_l), (cmp_parts, cmp_high, cmp_l)):
                level = lax.broadcasted_iota(jnp.int32, (levels, tr_dev), 0)
                parts.append(jnp.where(level.astype(jnp.float32) == index, 1.0, 0.0))
            so_parts = so_parts + [jnp.ones((8, tr_dev), jnp.float32)]
        join = lambda parts: jnp.concatenate(parts, axis=0).astype(jnp.bfloat16)
        rec_sum = dot_nt(join(rec_parts), rec_hot)
        cmp_sum = dot_nt(join(cmp_parts), cmp_hot)
        so_sum = dot_nt(join(so_parts), so_hot)
        rec_acc[...] += rec_sum[: rec_acc.shape[0]]
        cmp_acc[...] += cmp_sum[: cmp_acc.shape[0]]
        if first:
            rec_cnt[...] += rec_sum[rec_acc.shape[0] :]
            cmp_cnt[...] += cmp_sum[cmp_acc.shape[0] :]
            so_acc[src, :, 0:ITEMS] = so_sum
        else:
            so_acc[src, 0 : main + 2 * REM, 0:ITEMS] += so_sum

    order = [0, 1, 3, 2] if groups == 4 else [0]

    def first_pass(mask):
        @pl.loop(0, dests)
        def _(step):
            src = (my_group ^ mask) * dests + (my_place + dests - step) % dests
            if mask == 0:

                @pl.when(step > 0)
                def _():
                    block_copy(src, src).wait_recv()

            else:
                block_copy(src, src).wait_recv()
            add_source(src, True)

    for mask in order:
        first_pass(mask)

    held = main + 2 * REM

    def so_terms():
        sums = so_acc[...].reshape(n_shot, n_off, so_acc.shape[1], LANES)
        bins = jnp.sum(sums, axis=0)
        shots = jnp.sum(sums, axis=1)
        lane = lax.broadcasted_iota(jnp.int32, sums.shape, 3)
        both = jnp.where(lane < OFFB_DEV, bins[None], shots[:, None])
        both = both.reshape(so_acc.shape)
        return OMEGA * both[:, :held] / (both[:, held : held + 1] + 1.0)

    def scaled(acc, cnt, cols):
        levels = cnt.shape[0]
        width = cols.stop - cols.start
        low = lower_half((2 * REM, width))

        def main_part(l):
            return acc[l * main : (l + 1) * main, cols] * cnt[l : l + 1, cols]

        def pair_part(pair):
            scale = jnp.where(low, cnt[2 * pair + 1 : 2 * pair + 2, cols], cnt[2 * pair : 2 * pair + 1, cols])
            start = levels * main + 2 * REM * pair
            return acc[start : start + 2 * REM, cols] * scale

        return main_part, pair_part

    rec_cnt[...] = OMEGA / (rec_cnt[...] + 1.0)
    cmp_cnt[...] = OMEGA / (cmp_cnt[...] + 1.0)

    def refresh(x, acc, cnt):
        levels = cnt.shape[0]
        main_part, pair_part = scaled(acc, cnt, slice(0, WIDE))
        parts = [main_part(l) for l in range(levels)] if main else []
        parts += [pair_part(pair) for pair in range(levels // 2)]
        x[...] = jnp.concatenate(parts, axis=0).astype(jnp.bfloat16)

    for _ in range(SWEEPS - 1):
        refresh(rec_x, rec_acc, rec_cnt)
        refresh(cmp_x, cmp_acc, cmp_cnt)
        so = so_terms()
        so_high = so.astype(jnp.bfloat16).astype(jnp.float32)
        so_x[...] = jnp.concatenate([so_high, so - so_high], axis=1).astype(jnp.bfloat16)

        @pl.loop(0, n_dev)
        def _(src):
            add_source(src, False)

    so = so_terms()
    lane8 = lax.broadcasted_iota(jnp.int32, (8, LANES), 1)
    low8 = lower_half((8, LANES))

    def at_zero(values, offset):
        return values if offset == 0 else pltpu.roll(values, LANES - offset, 1)

    for dest in range(n_dev):
        cmp_level, cmp_at = divmod(dest * cmp_rows, WIDE)
        rec_level, rec_at = divmod(dest * rec_rows, WIDE)
        cmp_from, cmp_off = divmod(cmp_at, LANES)
        rec_from, rec_off = divmod(rec_at, LANES)
        cmp_main, cmp_pair = scaled(cmp_acc, cmp_cnt, slice(cmp_from * LANES, (cmp_from + 1) * LANES))
        rec_main, rec_pair = scaled(rec_acc, rec_cnt, slice(rec_from * LANES, (rec_from + 1) * LANES))
        extra = pltpu.roll(so[dest], rec_rows, 1)
        if main:
            ret_stage[dest, :main, :] = at_zero(cmp_main(cmp_level), cmp_off).astype(jnp.bfloat16)
            values = at_zero(rec_main(rec_level), rec_off)
            lane = lax.broadcasted_iota(jnp.int32, values.shape, 1)
            values = jnp.where(lane < rec_rows, values, extra[:main])
            ret_stage[dest, main + 8 :, :] = values.astype(jnp.bfloat16)
        cmp_rest = at_zero(cmp_pair(cmp_level // 2), cmp_off)
        if cmp_level % 2 == 1:
            cmp_rest = pltpu.roll(cmp_rest, REM, 0)
        rec_rest = at_zero(rec_pair(rec_level // 2), rec_off)
        if rec_level % 2 == 0:
            rec_rest = pltpu.roll(rec_rest, REM, 0)
        rec_rest = jnp.where(lane8 < rec_rows, rec_rest, extra[main:])
        ret_stage[dest, main : main + 8, :] = jnp.where(low8, rec_rest, cmp_rest).astype(jnp.bfloat16)

    own = pltpu.make_async_copy(ret_stage.at[me], ret_landed.at[me], own_sems.at[1])
    own.start()
    for mask in (3, 2, 1, 0) if groups == 4 else (0,):

        @pl.loop(1 if mask == 0 else 0, dests)
        def _(step):
            return_copy((my_group ^ mask) * dests + (step + my_place) % dests, me).start()

    @pl.loop(1, n_dev)
    def _(step):
        dest = (me + step) % n_dev
        block_copy(dest, me).wait_send()

    for step in range(1, groups):
        line_copy(step, my_group).wait_send()

    @pl.loop(1, dests)
    def _(step):
        layer_copy((my_place + step) % dests, my_place).wait_send()

    own.wait()

    @pl.loop(1, n_dev)
    def _(step):
        dest = (me + step) % n_dev
        return_copy(dest, me).wait_send()
        return_copy(dest, dest).wait_recv()

    out_ref[...] = ret_landed[...]


def run_terms(traces, ids, owners, sizes, held):
    n_shot, n_off, shot_dev, tr_off, rec_dev, cmp_dev, main = sizes
    n_dev = n_shot * n_off
    tr_dev, samples = traces.shape
    groups = group_count(n_dev)
    dests = n_dev // groups
    rows = dests * (main + REM)
    rec_l = owners[0].shape[0] // WIDE
    cmp_l = owners[2].shape[0] // WIDE
    tables = base_angles(samples, n_dev, held, main)
    vmem = pl.BlockSpec(memory_space=pltpu.VMEM)
    block = (n_dev, 2 * main + 2 * REM, tr_dev // 2)
    ret_block = (n_dev, 2 * main + 8, LANES)
    hot_bytes = n_dev * 2 * WIDE * tr_dev * 2
    kept = n_dev if hot_bytes <= HOT_BYTES else 1
    count = main + REM
    return pl.pallas_call(
        lambda *refs: terms_kernel(sizes, *refs),
        out_shape=jax.ShapeDtypeStruct(ret_block, jnp.bfloat16),
        in_specs=[vmem] * 13,
        out_specs=vmem,
        scratch_shapes=[
            pltpu.VMEM(block, jnp.bfloat16),
            pltpu.VMEM(block, jnp.bfloat16),
            pltpu.VMEM((2 * rows, samples), jnp.bfloat16),
            pltpu.VMEM((8, tr_dev), jnp.int32),
            pltpu.VMEM((ID_ROWS, tr_dev), jnp.float32),
            pltpu.VMEM((dests, groups, ID_ROWS, tr_dev), jnp.bfloat16),
            pltpu.VMEM((2 * rec_l, WIDE), jnp.float32),
            pltpu.VMEM((2 * cmp_l, WIDE), jnp.float32),
            pltpu.VMEM((WIDE, LANES), jnp.bfloat16),
            pltpu.VMEM((kept, 2, WIDE, tr_dev), jnp.bfloat16),
            pltpu.VMEM((rec_l * count, WIDE), jnp.float32),
            pltpu.VMEM((cmp_l * count, WIDE), jnp.float32),
            pltpu.VMEM((rec_l, WIDE), jnp.float32),
            pltpu.VMEM((cmp_l, WIDE), jnp.float32),
            pltpu.VMEM((n_dev, main + 2 * REM + 8, LANES), jnp.float32),
            pltpu.VMEM((rec_l * count, WIDE), jnp.bfloat16),
            pltpu.VMEM((cmp_l * count, WIDE), jnp.bfloat16),
            pltpu.VMEM((n_dev, 2 * (main + 2 * REM), LANES), jnp.bfloat16),
            pltpu.VMEM(ret_block, jnp.bfloat16),
            pltpu.VMEM(ret_block, jnp.bfloat16),
            pltpu.SemaphoreType.DMA((n_dev,)),
            pltpu.SemaphoreType.DMA((n_dev,)),
            pltpu.SemaphoreType.DMA((groups,)),
            pltpu.SemaphoreType.DMA((groups,)),
            pltpu.SemaphoreType.DMA((dests,)),
            pltpu.SemaphoreType.DMA((dests,)),
            pltpu.SemaphoreType.DMA((n_dev,)),
            pltpu.SemaphoreType.DMA((n_dev,)),
            pltpu.SemaphoreType.DMA((2,)),
        ],
        compiler_params=pltpu.CompilerParams(
            vmem_limit_bytes=VMEM_BYTES, collective_id=0, has_side_effects=True
        ),
        name="terms",
    )(traces, *ids, *tables, *owners)


def output_kernel(sizes, held, blocks_ref, source_ref, offset_ref, rec_ref, cmp_ref, joined):
    shot_dev, rec_rows, cmp_rows, main = sizes
    n_dev = blocks_ref.shape[0]
    for src in range(n_dev):
        rows = min(held, NF - src * held)
        if rows > 0:
            block = blocks_ref[src].astype(jnp.float32)
            start = src * held
            joined[start : start + rows, :LANES] = block[:rows]
            first = min(main, rows)
            if first:
                joined[start : start + first, LANES:] = block[main + 8 : main + 8 + first]
            if rows > main:
                joined[start + main : start + rows, LANES:] = block[main + REM : REM + rows]
    turned = joined[...].T
    cmp_ref[...] = turned[:cmp_rows]
    rec_ref[...] = turned[LANES : LANES + rec_rows]
    base = LANES + rec_rows
    offset_ref[...] = turned[base : base + OFFB_DEV]
    source_ref[...] = turned[base + OFFB_DEV : base + OFFB_DEV + shot_dev]


def write_outputs(blocks, sizes, held):
    shot_dev, rec_rows, cmp_rows, main = sizes
    vmem = pl.BlockSpec(memory_space=pltpu.VMEM)
    shape = lambda rows: jax.ShapeDtypeStruct((rows, NF), jnp.float32)
    return pl.pallas_call(
        lambda *refs: output_kernel(sizes, held, *refs),
        out_shape=(shape(shot_dev), shape(OFFB_DEV), shape(rec_rows), shape(cmp_rows)),
        in_specs=[vmem],
        out_specs=(vmem,) * 4,
        scratch_shapes=[pltpu.VMEM((NF, 2 * LANES), jnp.float32)],
        compiler_params=pltpu.CompilerParams(vmem_limit_bytes=VMEM_BYTES),
        name="outputs",
    )(blocks)


def shards(traces, offset_bin, rec_id, cmp_id, rec_owner, rec_slot, cmp_owner, cmp_slot):
    shot_dev, tr_off, samples = traces.shape
    n_shot = lax.axis_size("shot")
    n_off = lax.axis_size("off")
    n_dev = n_shot * n_off
    tr_dev = shot_dev * tr_off
    rec_dev = rec_owner.shape[0] // n_shot
    cmp_dev = cmp_owner.shape[0] // n_shot
    held = up(NF, n_dev) // n_dev
    main = up(max(held - REM, 0), 8)
    blocks = run_terms(
        traces.reshape(tr_dev, samples),
        (offset_bin, rec_id, cmp_id),
        (rec_owner, rec_slot, cmp_owner, cmp_slot),
        (n_shot, n_off, shot_dev, tr_off, rec_dev, cmp_dev, main),
        held,
    )
    sizes = (shot_dev, rec_dev // n_off, cmp_dev // n_off, main)
    return write_outputs(blocks, sizes, held)


def solution(mesh):
    return jax.shard_map(
        shards,
        mesh=mesh,
        in_specs=(
            P("shot", "off", None),
            P("shot", "off"),
            P("shot", "off"),
            P("shot", "off"),
            P(),
            P(),
            P(),
            P(),
        ),
        out_specs=(
            P("shot", None),
            P("off", None),
            P(("shot", "off"), None),
            P(("shot", "off"), None),
        ),
        check_vma=False,
    )
```

time: 109 us -> 83.2 us (0.76)
  Pallas kernels: 101 us -> 82.4 us
  local copies, waits for them, and re-layouts: 5.95 us -> 0 us
    pallas_call x2, Pallas kernels: 101 us -> 82.4 us  [the longest x1 80.4 us: run_terms(): pl.pallas_call(lambda *refs: terms_kernel(sizes, *refs), out_shape=jax.Sh...]
    unnamed x4 -> x0, local copies, waits for them, and re-layouts: 5.95 us -> none
where the time goes in v1:
time: 83.2 us; the launch traced here: 83 us
  Pallas kernels  82.4 us (99%)
    pallas_call x1, Pallas kernels, run_terms(): pl.pallas_call(lambda *refs: terms_kernel(sizes, *refs), out_shape=jax.Sh...  80.4 us
    pallas_call x1, Pallas kernels, write_outputs(): pl.pallas_call(lambda *refs: output_kernel(sizes, held, *refs), out_shape...  1.99 us

profile of v1, /device:TPU:0, one launch (start us, length us, event | category | flops | bytes accessed | tf_op | source)
XLA Modules:
  0.0 83.0 jit_solution(10594315918780522994)
XLA Ops:
  0.6 80.4 %terms.1.refs_0_ = bf16[32,40,128]{2,1,0:T(8,128)(2,1)} custom-call(bf16[768,2048]{1,0:T(8,128)(2,1)} %bitcast.1, s32[4,192]{1,0:T(4,128)} %refs_1_.1, s32[4,192]{1,0:T(4,128)} %refs_2_.1, s32[4,192]{1,0:T(4,128)} %refs_3_.1, f32[640,16]{1,0:T(8,128)} %constant.10.clone.refs_4_, f32[640,16]{1,0:T(8,128)} %constant.11.clone.refs_5_, ...), custom_call_target="tpu_custom_call" | custom-call | tf_op jit(solution)/shard_map/terms/pallas_call | solution.py:546
  81.0 2.0 %outputs.1 = (f32[4,640]{1,0:T(4,128)}, f32[8,640]{1,0:T(8,128)}, f32[64,640]{1,0:T(8,128)}, f32[128,640]{1,0:T(8,128)}) custom-call(bf16[32,40,128]{2,1,0:T(8,128)(2,1)} %terms.1.refs_0_), custom_call_target="tpu_custom_call" | custom-call | tf_op jit(solution)/shard_map/outputs/pallas_call | solution.py:615

commit v2 on v1

--- a/solution.py
+++ b/solution.py
@@ -92,6 +92,36 @@
 
 def fold(values):
     return values + pltpu.roll(values, REM, 0)
+
+
+def plan_of(groups, dests):
+    half = dests // 2
+    if groups != 4:
+        return [
+            ("logs", 0, 0, 0),
+            ("layer", 0, 0, 0),
+            ("send", 0, 0, dests),
+            ("settle", 0, 0, 0),
+            ("add", 0, 0, dests),
+        ]
+    return [
+        ("logs", 3, 0, 0),
+        ("send", 3, 0, half),
+        ("layer", 0, 0, 0),
+        ("logs", 2, 0, 0),
+        ("send", 3, half, dests),
+        ("send", 2, 0, half),
+        ("logs", 0, 0, 0),
+        ("send", 0, 0, dests),
+        ("logs", 1, 0, 0),
+        ("settle", 0, 0, 0),
+        ("send", 2, half, dests),
+        ("add", 0, 0, dests),
+        ("send", 1, 0, dests),
+        ("add", 3, 0, dests),
+        ("add", 1, 0, dests),
+        ("add", 2, 0, dests),
+    ]
 
 
 def terms_kernel(
@@ -214,11 +244,6 @@
             stage[first + 2 * pair, 2 * main :, :] = upper.astype(jnp.bfloat16)
             stage[first + 2 * pair + 1, 2 * main :, :] = lower.astype(jnp.bfloat16)
 
-    def send_group(group, own):
-        @pl.loop(1 if own else 0, dests)
-        def _(step):
-            block_copy(group * dests + (step + my_place) % dests, me).start()
-
     def one_hot_f32(index):
         row = lax.broadcasted_iota(jnp.int32, (WIDE, index.shape[1]), 0)
         return jnp.where(row == index, 1.0, 0.0).astype(jnp.bfloat16)
@@ -273,26 +298,9 @@
     cmp_cnt[...] = jnp.zeros_like(cmp_cnt)
     so_acc[...] = jnp.zeros_like(so_acc)
 
-    turns = [3, 0, 2, 1] if groups == 4 else [0]
-    for turn, mask in enumerate(turns):
-        stage_logs(my_group ^ mask)
-        if turn == 0:
-            pl.semaphore_wait(barrier, n_dev - 1)
-        send_group(my_group ^ mask, mask == 0)
-        if turn == 0:
-            own_ids()
-            send_line()
-        if turn == min(1, groups - 1):
-            send_layer()
-    own = pltpu.make_async_copy(stage.at[me], landed.at[me], own_sems.at[0])
-    own.start()
-    own.wait()
-
-    @pl.loop(1, dests)
-    def _(step):
-        place = (my_place + dests - step) % dests
-        layer_copy(place, place).wait_recv()
-
+    own_ids()
+    pl.semaphore_wait(barrier, n_dev - 1)
+    send_line()
     chunks = main // 8
     low_full = lower_half((2 * REM, tr_dev))
     low_half = lower_half((2 * REM, half))
@@ -300,15 +308,22 @@
     item_row = lax.broadcasted_iota(jnp.int32, (ITEMS, tr_dev), 0)
     shot_hot = item_row - OFFB_DEV == local_shot
 
+    row_base = lax.broadcasted_iota(jnp.int32, (16, LANES), 0).astype(jnp.float32)
+    row_base = row_base.astype(jnp.bfloat16)
+
     def make_hot(index):
-        column = index.astype(jnp.bfloat16)
+        column = jnp.broadcast_to(index, (16, tr_dev)).astype(jnp.bfloat16)
         one = jnp.ones((), jnp.bfloat16)
         zero = jnp.zeros((), jnp.bfloat16)
         parts = []
-        for a in range(tr_dev // LANES):
-            cols = slice(a * LANES, (a + 1) * LANES)
-            parts.append(jnp.where(iota_ref[...] == column[:, cols], one, zero))
-        return jnp.concatenate(parts, axis=1)
+        for i in range(WIDE // 16):
+            row = row_base + jnp.full((), 16 * i, jnp.bfloat16)
+            pieces = []
+            for a in range(tr_dev // LANES):
+                piece = column[:, a * LANES : (a + 1) * LANES]
+                pieces.append(jnp.where(row == piece, one, zero))
+            parts.append(jnp.concatenate(pieces, axis=1))
+        return jnp.concatenate(parts, axis=0)
 
     def level_masks(index, levels):
         level = jnp.broadcast_to(index, (8, tr_dev))
@@ -400,13 +415,21 @@
         else:
             so_acc[src, 0 : main + 2 * REM, 0:ITEMS] += so_sum
 
-    order = [0, 1, 3, 2] if groups == 4 else [0]
-
-    def first_pass(mask):
-        @pl.loop(0, dests)
+    def send_part(mask, low, high):
+        @pl.loop(max(low, 1) if mask == 0 else low, high)
+        def _(step):
+            block_copy((my_group ^ mask) * dests + (step + my_place) % dests, me).start()
+
+    def drain_part(mask, low, high):
+        @pl.loop(max(low, 1) if mask == 0 else low, high)
+        def _(step):
+            block_copy((my_group ^ mask) * dests + (step + my_place) % dests, me).wait_send()
+
+    def add_part(mask, low, high):
+        @pl.loop(low, high)
         def _(step):
             src = (my_group ^ mask) * dests + (my_place + dests - step) % dests
-            if mask == 0:
+            if mask == 0 and low == 0:
 
                 @pl.when(step > 0)
                 def _():
@@ -416,8 +439,30 @@
                 block_copy(src, src).wait_recv()
             add_source(src, True)
 
-    for mask in order:
-        first_pass(mask)
+    def settle_own():
+        own = pltpu.make_async_copy(stage.at[me], landed.at[me], own_sems.at[0])
+        own.start()
+        own.wait()
+
+        @pl.loop(1, dests)
+        def _(step):
+            place = (my_place + dests - step) % dests
+            layer_copy(place, place).wait_recv()
+
+    plan = plan_of(groups, dests)
+    for name, mask, low, high in plan:
+        if name == "logs":
+            stage_logs(my_group ^ mask)
+        elif name == "layer":
+            send_layer()
+        elif name == "send":
+            send_part(mask, low, high)
+        elif name == "drain":
+            drain_part(mask, low, high)
+        elif name == "settle":
+            settle_own()
+        else:
+            add_part(mask, low, high)
 
     held = main + 2 * REM
 
@@ -462,7 +507,7 @@
         so_high = so.astype(jnp.bfloat16).astype(jnp.float32)
         so_x[...] = jnp.concatenate([so_high, so - so_high], axis=1).astype(jnp.bfloat16)
 
-        @pl.loop(0, n_dev)
+        @pl.loop(0, n_dev, unroll=2)
         def _(src):
             add_source(src, False)
 
@@ -504,10 +549,11 @@
         def _(step):
             return_copy((my_group ^ mask) * dests + (step + my_place) % dests, me).start()
 
-    @pl.loop(1, n_dev)
-    def _(step):
-        dest = (me + step) % n_dev
-        block_copy(dest, me).wait_send()
+    drained = {(mask, step) for name, mask, low, high in plan if name == "drain" for step in range(low, high)}
+    for mask in range(groups):
+        left = [step for step in range(dests) if (mask, step) not in drained]
+        if left:
+            drain_part(mask, left[0], left[-1] + 1)
 
     for step in range(1, groups):
         line_copy(step, my_group).wait_send()

time: 83.2 us -> 73.3 us (0.88)
  Pallas kernels: 82.4 us -> 72.5 us
    pallas_call x1, Pallas kernels: 80.4 us -> 70.5 us  [run_terms(): pl.pallas_call(lambda *refs: terms_kernel(sizes, *refs), out_shape=jax.Sh...]
where the time goes in v2:
time: 73.3 us; the launch traced here: 73.2 us
  Pallas kernels  72.5 us (99%)
    pallas_call x1, Pallas kernels, run_terms(): pl.pallas_call(lambda *refs: terms_kernel(sizes, *refs), out_shape=jax.Sh...  70.5 us
    pallas_call x1, Pallas kernels, write_outputs(): pl.pallas_call(lambda *refs: output_kernel(sizes, held, *refs), out_shape...  1.99 us

profile of v2, /device:TPU:0, one launch (start us, length us, event | category | flops | bytes accessed | tf_op | source)
XLA Modules:
  0.0 73.2 jit_solution(5343182890936510693)
XLA Ops:
  0.6 70.5 %terms.1.refs_0_ = bf16[32,40,128]{2,1,0:T(8,128)(2,1)} custom-call(bf16[768,2048]{1,0:T(8,128)(2,1)} %bitcast.1, s32[4,192]{1,0:T(4,128)} %refs_1_.1, s32[4,192]{1,0:T(4,128)} %refs_2_.1, s32[4,192]{1,0:T(4,128)} %refs_3_.1, f32[640,16]{1,0:T(8,128)} %constant.10.clone.refs_4_, f32[640,16]{1,0:T(8,128)} %constant.11.clone.refs_5_, ...), custom_call_target="tpu_custom_call" | custom-call | tf_op jit(solution)/shard_map/terms/pallas_call | solution.py:592
  71.2 2.0 %outputs.1 = (f32[4,640]{1,0:T(4,128)}, f32[8,640]{1,0:T(8,128)}, f32[64,640]{1,0:T(8,128)}, f32[128,640]{1,0:T(8,128)}) custom-call(bf16[32,40,128]{2,1,0:T(8,128)(2,1)} %terms.1.refs_0_), custom_call_target="tpu_custom_call" | custom-call | tf_op jit(solution)/shard_map/outputs/pallas_call | solution.py:661

commit v3 on v2

--- a/solution.py
+++ b/solution.py
@@ -126,7 +126,7 @@
 
 def terms_kernel(
     sizes,
-    traces_ref,
+    traces_hbm,
     bin_ref,
     rec_ref,
     cmp_ref,
@@ -142,7 +142,8 @@
     out_ref,
     stage,
     landed,
-    table,
+    even_table,
+    odd_table,
     raw,
     id_rows,
     ids,
@@ -169,6 +170,7 @@
     ret_send_sems,
     ret_recv_sems,
     own_sems,
+    traces_ref,
 ):
     n_shot, n_off, shot_dev, tr_off, rec_dev, cmp_dev, main = sizes
     n_dev = n_shot * n_off
@@ -185,6 +187,8 @@
     me = lax.axis_index("shot") * n_off + lax.axis_index("off")
     my_group = me // dests
     my_place = me % dests
+    fetch = pltpu.make_async_copy(traces_hbm, traces_ref, own_sems.at[2])
+    fetch.start()
     barrier = greet_all(me, n_dev, n_off)
 
     def block_copy(dest, slot):
@@ -212,7 +216,7 @@
             n_off,
         )
 
-    def stage_logs(group):
+    def make_table(group, table):
         base = pl.multiple_of(group * rows, 8)
         cb = cb_ref[pl.ds(base, rows), :]
         sb = sb_ref[pl.ds(base, rows), :]
@@ -225,6 +229,13 @@
             sa = sa_all[:, a : a + 1]
             table[:rows, cols] = (w * (ca * cb - sa * sb)).astype(jnp.bfloat16)
             table[rows:, cols] = (-w * (sa * cb + ca * sb)).astype(jnp.bfloat16)
+
+    def stage_logs(group, turn, later):
+        table, spare = (even_table, odd_table) if turn % 2 == 0 else (odd_table, even_table)
+        if later is not None:
+            make_table(later, spare)
+        if turn == 0:
+            fetch.wait()
         products = dot_nt(table[...], traces_ref[...])
         real_part = products[:rows]
         imag_part = products[rows:]
@@ -298,6 +309,9 @@
     cmp_cnt[...] = jnp.zeros_like(cmp_cnt)
     so_acc[...] = jnp.zeros_like(so_acc)
 
+    plan = plan_of(groups, dests)
+    log_groups = [my_group ^ mask for name, mask, _, _ in plan if name == "logs"] + [None]
+    make_table(log_groups[0], even_table)
     own_ids()
     pl.semaphore_wait(barrier, n_dev - 1)
     send_line()
@@ -426,7 +440,7 @@
             block_copy((my_group ^ mask) * dests + (step + my_place) % dests, me).wait_send()
 
     def add_part(mask, low, high):
-        @pl.loop(low, high)
+        @pl.loop(low, high, unroll=4)
         def _(step):
             src = (my_group ^ mask) * dests + (my_place + dests - step) % dests
             if mask == 0 and low == 0:
@@ -449,10 +463,11 @@
             place = (my_place + dests - step) % dests
             layer_copy(place, place).wait_recv()
 
-    plan = plan_of(groups, dests)
+    turn = 0
     for name, mask, low, high in plan:
         if name == "logs":
-            stage_logs(my_group ^ mask)
+            stage_logs(my_group ^ mask, turn, log_groups[turn + 1])
+            turn += 1
         elif name == "layer":
             send_layer()
         elif name == "send":
@@ -507,7 +522,7 @@
         so_high = so.astype(jnp.bfloat16).astype(jnp.float32)
         so_x[...] = jnp.concatenate([so_high, so - so_high], axis=1).astype(jnp.bfloat16)
 
-        @pl.loop(0, n_dev, unroll=2)
+        @pl.loop(0, n_dev, unroll=4)
         def _(src):
             add_source(src, False)
 
@@ -592,11 +607,12 @@
     return pl.pallas_call(
         lambda *refs: terms_kernel(sizes, *refs),
         out_shape=jax.ShapeDtypeStruct(ret_block, jnp.bfloat16),
-        in_specs=[vmem] * 13,
+        in_specs=[pl.BlockSpec(memory_space=pl.ANY)] + [vmem] * 12,
         out_specs=vmem,
         scratch_shapes=[
             pltpu.VMEM(block, jnp.bfloat16),
             pltpu.VMEM(block, jnp.bfloat16),
+            pltpu.VMEM((2 * rows, samples), jnp.bfloat16),
             pltpu.VMEM((2 * rows, samples), jnp.bfloat16),
             pltpu.VMEM((8, tr_dev), jnp.int32),
             pltpu.VMEM((ID_ROWS, tr_dev), jnp.float32),
@@ -623,7 +639,8 @@
             pltpu.SemaphoreType.DMA((dests,)),
             pltpu.SemaphoreType.DMA((n_dev,)),
             pltpu.SemaphoreType.DMA((n_dev,)),
-            pltpu.SemaphoreType.DMA((2,)),
+            pltpu.SemaphoreType.DMA((3,)),
+            pltpu.VMEM((tr_dev, samples), jnp.bfloat16),
         ],
         compiler_params=pltpu.CompilerParams(
             vmem_limit_bytes=VMEM_BYTES, collective_id=0, has_side_effects=True

time: 73.3 us -> 70.6 us (0.963)
  Pallas kernels: 72.5 us -> 69.7 us
    pallas_call x1, Pallas kernels: 70.5 us -> 67.8 us  [run_terms(): pl.pallas_call(lambda *refs: terms_kernel(sizes, *refs), out_shape=jax.Sh...]
where the time goes in v3:
time: 70.6 us; the launch traced here: 70.4 us
  Pallas kernels  69.7 us (99%)
    pallas_call x1, Pallas kernels, run_terms(): pl.pallas_call(lambda *refs: terms_kernel(sizes, *refs), out_shape=jax.Sh...  67.8 us
    pallas_call x1, Pallas kernels, write_outputs(): pl.pallas_call(lambda *refs: output_kernel(sizes, held, *refs), out_shape...  1.99 us

profile of v3, /device:TPU:0, one launch (start us, length us, event | category | flops | bytes accessed | tf_op | source)
XLA Modules:
  0.0 70.4 jit_solution(7777366634411889702)
XLA Ops:
  0.6 67.8 %terms.1.refs_0_ = bf16[32,40,128]{2,1,0:T(8,128)(2,1)} custom-call(bf16[768,2048]{1,0:T(8,128)(2,1)} %bitcast.1, s32[4,192]{1,0:T(4,128)} %refs_1_.1, s32[4,192]{1,0:T(4,128)} %refs_2_.1, s32[4,192]{1,0:T(4,128)} %refs_3_.1, f32[640,16]{1,0:T(8,128)} %constant.10.clone.refs_4_, f32[640,16]{1,0:T(8,128)} %constant.11.clone.refs_5_, ...), custom_call_target="tpu_custom_call" | custom-call | tf_op jit(solution)/shard_map/terms/pallas_call | solution.py:607
  68.4 2.0 %outputs.1 = (f32[4,640]{1,0:T(4,128)}, f32[8,640]{1,0:T(8,128)}, f32[64,640]{1,0:T(8,128)}, f32[128,640]{1,0:T(8,128)}) custom-call(bf16[32,40,128]{2,1,0:T(8,128)(2,1)} %terms.1.refs_0_), custom_call_target="tpu_custom_call" | custom-call | tf_op jit(solution)/shard_map/outputs/pallas_call | solution.py:678
